TPU v7x, 32 devices: a whole 2x2x4 slice. The times are simulated.
32 devices in a mesh: dp: 2 (over y), seq: 8 (over z, x), tensor: 2 (over core).
Axes of the slice: x: 2, y: 2, z: 4, core: 2. Of those that a mesh axis runs over, the one named last changes fastest.
Arguments:
- tokens: bfloat16 [4, 8192, 512], P('dp', 'seq'), may hold values from -6 to 6
- segments: int32 [4, 8192], P('dp', 'seq'), may hold values from 0 to 15, never falling along the last dimension, each value on 1 to 5120 neighbouring positions
- keep_mask: int32 [4, 8192], P('dp', 'seq'), may hold values 0 or 1
- cotangent: bfloat16 [4, 8192, 512], P('dp', 'seq'), may hold values from -6 to 6
- ln1_gain: float32 [512], replicated, may hold values from 0.25 to 1.75
- ln1_bias: float32 [512], replicated, may hold values from -1.5 to 1.5
- w_qkv: bfloat16 [3, 512, 512], P(None, None, 'tensor'), may hold values from -0.25 to 0.25
- qv_bias: float32 [2, 512], P(None, 'tensor'), may hold values from -1.5 to 1.5
- w_out: bfloat16 [512, 512], P('tensor'), may hold values from -1.5 to 1.5
- b_out: float32 [512], replicated, may hold values from -1.5 to 1.5
- ln2_gain: float32 [512], replicated, may hold values from 0.25 to 1.75
- ln2_bias: float32 [512], replicated, may hold values from -1.5 to 1.5
- w_fc: bfloat16 [512, 2048], P(None, 'tensor'), may hold values from -0.25 to 0.25
- b_fc: float32 [2048], P('tensor'), may hold values from -1.5 to 1.5
- w_proj: bfloat16 [2048, 512], P('tensor'), may hold values from -0.125 to 0.125
- b_proj: float32 [512], replicated, may hold values from -1.5 to 1.5
Outputs:
- layer_out: bfloat16 [4, 8192, 512], P('dp', 'seq')
- grad_tokens: bfloat16 [4, 8192, 512], P('dp', 'seq')
- grad_ln1_gain: float32 [512], replicated
- grad_ln1_bias: float32 [512], replicated
- grad_w_qkv: float32 [3, 512, 512], P(None, None, 'tensor')
- grad_qv_bias: float32 [2, 512], P(None, 'tensor')
- grad_w_out: float32 [512, 512], P('tensor')
- grad_b_out: float32 [512], replicated
- grad_ln2_gain: float32 [512], replicated
- grad_ln2_bias: float32 [512], replicated
- grad_w_fc: float32 [512, 2048], P(None, 'tensor')
- grad_b_fc: float32 [2048], P('tensor')
- grad_w_proj: float32 [2048, 512], P('tensor')
- grad_b_proj: float32 [512], replicated
Inputs may be any that keep to these rules, and one draw needn't show every extreme that they name: `segments`: in each sequence the document numbers never fall; each document holds 1 to 5120 tokens, and one holds exactly 5120.
All inputs are finite; a program needn't handle non-finite values. No bound on the sum of `keep_mask` on one device may be relied on, other than what follows from the above.
Results may differ from a plain program's by a relative error of at most 0.024.
Values may be sent and summed in bfloat16 or wider, within the bound.
No kernel may reach another device: no remote copies, remote signals or barrier semaphores. Data moves between devices by JAX's collectives and lax.ppermute only.
A program may use at most 512 MiB of HBM per device.

v0:
```python
import jax
import jax.numpy as jnp
from jax import lax
from jax.sharding import PartitionSpec as P

HEAD_DIM = 64
EPSILON = 1e-05
MASKED = -1e30


def layer_norm(rows, gain, offset):
    centred = rows - jnp.mean(rows, -1, keepdims=True)
    rstd = lax.rsqrt(jnp.mean(centred * centred, -1, keepdims=True) + EPSILON)
    normed = centred * rstd
    return (normed * gain + offset, normed, rstd)


def norm_back(grad_norm, normed, rstd, gain):
    scaled = grad_norm * gain
    return rstd * (
        scaled
        - jnp.mean(scaled, -1, keepdims=True)
        - normed * jnp.mean(scaled * normed, -1, keepdims=True)
    )


def gelu_parts(pre_act):
    sigma = jax.nn.sigmoid(1.702 * pre_act)
    return (pre_act * sigma, sigma + 1.702 * pre_act * sigma * (1.0 - sigma))


def visible(query_pos, query_seg, key_pos, key_seg, key_keep):
    allowed = (query_seg[:, None] == key_seg[None, :]) & (key_pos[None, :] <= query_pos[:, None])
    return allowed & ((key_keep[None, :] == 1) | (key_pos[None, :] == query_pos[:, None]))


def on_device(
    tokens,
    segments,
    keep_mask,
    cotangent,
    ln1_gain,
    ln1_bias,
    w_qkv,
    qv_bias,
    w_out,
    b_out,
    ln2_gain,
    ln2_bias,
    w_fc,
    b_fc,
    w_proj,
    b_proj,
):
    sequences, group_rows, width = tokens.shape
    local_width = w_qkv.shape[2]
    heads_here = local_width // HEAD_DIM
    score_scale = HEAD_DIM ** (-0.5)
    seg_all, keep_all = (
        lax.all_gather(segments, "seq", axis=1, tiled=True),
        lax.all_gather(keep_mask, "seq", axis=1, tiled=True),
    )
    full_length = seg_all.shape[1]
    key_block = min(512, full_length)
    block_count = full_length // key_block
    piece_index = lax.axis_index("seq")
    query_pos = piece_index * group_rows + jnp.arange(group_rows, dtype=jnp.int32)
    params = (
        ln1_gain,
        ln1_bias,
        w_qkv,
        qv_bias,
        w_out,
        b_out,
        ln2_gain,
        ln2_bias,
        w_fc,
        b_fc,
        w_proj,
        b_proj,
    )
    sums = [jnp.zeros(p.shape, jnp.float32) for p in params]
    outputs = []
    input_grads = []
    for sequence_index in range(sequences):
        rows = tokens[sequence_index].astype(jnp.float32)
        seg_row = seg_all[sequence_index]
        keep_row = keep_all[sequence_index]
        query_seg = segments[sequence_index]
        normed_one_out, normed_one, rstd_one = layer_norm(rows, ln1_gain, ln1_bias)
        hidden_one = normed_one_out.astype(jnp.bfloat16)
        projected = jnp.einsum("te,ced->ctd", hidden_one, w_qkv, preferred_element_type=jnp.float32)
        queries = (projected[0] + qv_bias[0]).astype(jnp.bfloat16)
        keys = projected[1].astype(jnp.bfloat16)
        values = (projected[2] + qv_bias[1]).astype(jnp.bfloat16)
        query_heads = queries.reshape(group_rows, heads_here, HEAD_DIM)
        best = jnp.full((heads_here, group_rows), MASKED, jnp.float32)
        key_part = lax.all_gather(keys, "seq", axis=0, tiled=True)
        value_part = lax.all_gather(values, "seq", axis=0, tiled=True)
        row_count = key_part.shape[0]
        key_pos = jnp.arange(row_count, dtype=jnp.int32)
        key_seg = seg_row
        key_keep = keep_row
        allowed = visible(query_pos, query_seg, key_pos, key_seg, key_keep)[None]
        scores = (
            jnp.einsum(
                "qhd,khd->hqk",
                query_heads,
                key_part.reshape(row_count, heads_here, HEAD_DIM),
                preferred_element_type=jnp.float32,
            )
            * score_scale
        )
        scores = jnp.where(allowed, scores, MASKED)
        new_best = jnp.maximum(best, jnp.max(scores, -1))
        weights = jnp.where(allowed, jnp.exp(scores - new_best[..., None]), 0.0)
        weight_sum = jnp.sum(weights, -1)
        accum = jnp.einsum(
            "hqk,khd->hqd",
            weights.astype(jnp.bfloat16),
            value_part.reshape(row_count, heads_here, HEAD_DIM),
            preferred_element_type=jnp.float32,
        )
        best, weight_sum, accum = (new_best, weight_sum, accum)
        log_sum = best + jnp.log(weight_sum)
        attn_out = (
            (accum / weight_sum[..., None])
            .transpose(1, 0, 2)
            .reshape(group_rows, local_width)
            .astype(jnp.bfloat16)
        )
        attn_term = jnp.dot(attn_out, w_out, preferred_element_type=jnp.float32)
        middle = (
            rows + lax.psum(attn_term.astype(jnp.bfloat16), "tensor").astype(jnp.float32) + b_out
        )
        normed_two_out, normed_two, rstd_two = layer_norm(middle, ln2_gain, ln2_bias)
        hidden_two = normed_two_out.astype(jnp.bfloat16)
        pre_act = jnp.dot(hidden_two, w_fc, preferred_element_type=jnp.float32) + b_fc
        activated, slope = gelu_parts(pre_act)
        act_low = activated.astype(jnp.bfloat16)
        feed_term = jnp.dot(act_low, w_proj, preferred_element_type=jnp.float32)
        feed = lax.psum(feed_term.astype(jnp.bfloat16), "tensor").astype(jnp.float32) + b_proj
        outputs.append((middle + feed).astype(jnp.bfloat16))
        grad_out = cotangent[sequence_index]
        grad_out_wide = grad_out.astype(jnp.float32)
        sums[11] = sums[11] + jnp.sum(grad_out_wide, 0)
        sums[10] = sums[10] + jnp.einsum(
            "tf,td->fd", act_low, grad_out, preferred_element_type=jnp.float32
        )
        grad_act = jnp.einsum("td,fd->tf", grad_out, w_proj, preferred_element_type=jnp.float32)
        grad_pre = (grad_act * slope).astype(jnp.bfloat16)
        sums[9] = sums[9] + jnp.sum(grad_pre.astype(jnp.float32), 0)
        sums[8] = sums[8] + jnp.einsum(
            "te,tf->ef", hidden_two, grad_pre, preferred_element_type=jnp.float32
        )
        grad_hidden_two = lax.psum(
            jnp.einsum("tf,ef->te", grad_pre, w_fc, preferred_element_type=jnp.float32).astype(
                jnp.bfloat16
            ),
            "tensor",
        ).astype(jnp.float32)
        sums[6] = sums[6] + jnp.sum(grad_hidden_two * normed_two, 0)
        sums[7] = sums[7] + jnp.sum(grad_hidden_two, 0)
        grad_middle = grad_out_wide + norm_back(grad_hidden_two, normed_two, rstd_two, ln2_gain)
        grad_branch = grad_middle.astype(jnp.bfloat16)
        sums[5] = sums[5] + jnp.sum(grad_branch.astype(jnp.float32), 0)
        sums[4] = sums[4] + jnp.einsum(
            "tc,td->cd", attn_out, grad_branch, preferred_element_type=jnp.float32
        )
        grad_mixed = jnp.einsum(
            "td,cd->tc", grad_branch, w_out, preferred_element_type=jnp.float32
        ).astype(jnp.bfloat16)
        grad_heads = grad_mixed.reshape(group_rows, heads_here, HEAD_DIM)
        row_dot = jnp.sum(
            (grad_mixed.astype(jnp.float32) * attn_out.astype(jnp.float32)).reshape(
                group_rows, heads_here, HEAD_DIM
            ),
            -1,
        ).T
        key_use, value_use = (
            lax.all_gather(keys, "seq", axis=0, tiled=True),
            lax.all_gather(values, "seq", axis=0, tiled=True),
        )

        def make_step(key_src, value_src, seg_src, keep_src, pos_base, block_rows):

            def key_step(grad_query_sum, block_index):
                first_row = block_index * block_rows
                key_part = lax.dynamic_slice_in_dim(key_src, first_row, block_rows).reshape(
                    block_rows, heads_here, HEAD_DIM
                )
                value_part = lax.dynamic_slice_in_dim(value_src, first_row, block_rows).reshape(
                    block_rows, heads_here, HEAD_DIM
                )
                key_pos = pos_base + first_row + jnp.arange(block_rows, dtype=jnp.int32)
                key_seg = lax.dynamic_slice_in_dim(seg_src, first_row, block_rows)
                key_keep = lax.dynamic_slice_in_dim(keep_src, first_row, block_rows)
                allowed = visible(query_pos, query_seg, key_pos, key_seg, key_keep)[None]
                scores = (
                    jnp.einsum(
                        "qhd,khd->hqk", query_heads, key_part, preferred_element_type=jnp.float32
                    )
                    * score_scale
                )
                probs = jnp.where(allowed, jnp.exp(scores - log_sum[..., None]), 0.0)
                grad_probs = jnp.einsum(
                    "qhd,khd->hqk", grad_heads, value_part, preferred_element_type=jnp.float32
                )
                grad_scores = (probs * (grad_probs - row_dot[..., None])).astype(jnp.bfloat16)
                grad_query_sum = grad_query_sum + jnp.einsum(
                    "hqk,khd->qhd", grad_scores, key_part, preferred_element_type=jnp.float32
                )
                key_term = jnp.einsum(
                    "hqk,qhd->khd", grad_scores, query_heads, preferred_element_type=jnp.float32
                )
                value_term = jnp.einsum(
                    "hqk,qhd->khd",
                    probs.astype(jnp.bfloat16),
                    grad_heads,
                    preferred_element_type=jnp.float32,
                )
                return (
                    grad_query_sum,
                    (
                        key_term.reshape(block_rows, local_width),
                        value_term.reshape(block_rows, local_width),
                    ),
                )

            return key_step

        query_start = jnp.zeros((group_rows, heads_here, HEAD_DIM), jnp.float32)
        step_fn = make_step(key_use, value_use, seg_row, keep_row, 0, key_block)
        grad_query_sum, (key_terms, value_terms) = lax.scan(
            step_fn, query_start, jnp.arange(block_count, dtype=jnp.int32)
        )
        key_terms = key_terms.reshape(full_length, local_width) * score_scale
        value_terms = value_terms.reshape(full_length, local_width)
        key_grads, value_grads = (
            lax.psum_scatter(
                key_terms.astype(jnp.bfloat16), "seq", scatter_dimension=0, tiled=True
            ).astype(jnp.float32),
            lax.psum_scatter(
                value_terms.astype(jnp.bfloat16), "seq", scatter_dimension=0, tiled=True
            ).astype(jnp.float32),
        )
        grad_queries = (
            (grad_query_sum * score_scale).reshape(group_rows, local_width).astype(jnp.bfloat16)
        )
        value_low = value_grads.astype(jnp.bfloat16)
        stacked = jnp.stack([grad_queries, key_grads.astype(jnp.bfloat16), value_low])
        sums[2] = sums[2] + jnp.einsum(
            "te,ctd->ced", hidden_one, stacked, preferred_element_type=jnp.float32
        )
        sums[3] = sums[3] + jnp.stack(
            [
                jnp.sum(grad_queries.astype(jnp.float32), 0),
                jnp.sum(value_low.astype(jnp.float32), 0),
            ]
        )
        grad_hidden_one = lax.psum(
            jnp.einsum("ctd,ced->te", stacked, w_qkv, preferred_element_type=jnp.float32).astype(
                jnp.bfloat16
            ),
            "tensor",
        ).astype(jnp.float32)
        sums[0] = sums[0] + jnp.sum(grad_hidden_one * normed_one, 0)
        sums[1] = sums[1] + jnp.sum(grad_hidden_one, 0)
        grad_rows = grad_middle + norm_back(grad_hidden_one, normed_one, rstd_one, ln1_gain)
        input_grads.append(grad_rows.astype(jnp.bfloat16))
    totals = (
        lax.psum(sums[0].astype(jnp.bfloat16), ("dp", "seq")).astype(jnp.float32),
        lax.psum(sums[1].astype(jnp.bfloat16), ("dp", "seq")).astype(jnp.float32),
        lax.psum(sums[2].astype(jnp.bfloat16), ("dp", "seq")).astype(jnp.float32),
        lax.psum(sums[3].astype(jnp.bfloat16), ("dp", "seq")).astype(jnp.float32),
        lax.psum(sums[4].astype(jnp.bfloat16), ("dp", "seq")).astype(jnp.float32),
        lax.psum(sums[5].astype(jnp.bfloat16), ("dp", "seq")).astype(jnp.float32),
        lax.psum(sums[6].astype(jnp.bfloat16), ("dp", "seq")).astype(jnp.float32),
        lax.psum(sums[7].astype(jnp.bfloat16), ("dp", "seq")).astype(jnp.float32),
        lax.psum(sums[8].astype(jnp.bfloat16), ("dp", "seq")).astype(jnp.float32),
        lax.psum(sums[9].astype(jnp.bfloat16), ("dp", "seq")).astype(jnp.float32),
        lax.psum(sums[10].astype(jnp.bfloat16), ("dp", "seq")).astype(jnp.float32),
        lax.psum(sums[11].astype(jnp.bfloat16), ("dp", "seq")).astype(jnp.float32),
    )
    return (
        jnp.stack(outputs),
        jnp.stack(input_grads),
        totals[0],
        totals[1],
        totals[2],
        totals[3],
        totals[4],
        totals[5],
        totals[6],
        totals[7],
        totals[8],
        totals[9],
        totals[10],
        totals[11],
    )


def solution(mesh):
    return jax.shard_map(
        on_device,
        mesh=mesh,
        in_specs=(
            P("dp", "seq", None),
            P("dp", "seq"),
            P("dp", "seq"),
            P("dp", "seq", None),
            P(),
            P(),
            P(None, None, "tensor"),
            P(None, "tensor"),
            P("tensor", None),
            P(),
            P(),
            P(),
            P(None, "tensor"),
            P("tensor"),
            P("tensor", None),
            P(),
        ),
        out_specs=(
            P("dp", "seq", None),
            P("dp", "seq", None),
            P(),
            P(),
            P(None, None, "tensor"),
            P(None, "tensor"),
            P("tensor", None),
            P(),
            P(),
            P(),
            P(None, "tensor"),
            P("tensor"),
            P("tensor", None),
            P(),
        ),
        check_vma=False,
    )
```

profile of v0, /device:TPU:0, one launch (start us, length us, event | category | flops | bytes accessed | tf_op | source)
XLA Modules:
  0.0 1566.7 jit_solution(10269686080167025364)
XLA Ops:
  23.1 32.7 %all_gather.22 = s32[2,8192]{1,0:T(2,128)S(1)} all-gather(s32[2,1024]{1,0:T(2,128)S(1)} %copy-done.84), channel_id=1, replica_groups=mesh['dp'=2,'seq'=8,'tensor'=2] {'seq'}, dimensions={1}, use_global_device_ids=true | all-gather | bytes 73728 | tf_op jit(solution)/shard_map/all_gather | solution.py:60
  58.3 31.5 %all_gather.23 = s32[2,8192]{1,0:T(2,128)S(1)} all-gather(s32[2,1024]{1,0:T(2,128)S(1)} %copy-done.89), channel_id=1, replica_groups=mesh['dp'=2,'seq'=8,'tensor'=2] {'seq'}, dimensions={1}, use_global_device_ids=true | all-gather | bytes 73728 | tf_op jit(solution)/shard_map/all_gather | solution.py:61
  92.1 24.5 %fusion.37 = (pred[1024,8192]{1,0:T(8,128)(4,1)}, pred[1024,8192]{1,0:T(8,128)(4,1)}) fusion(s32[8192]{0:T(1024)S(1)} %bitcast.455, s32[1024]{0:T(1024)S(1)} %iota_add_fusion.4, s32[1024]{0:T(1024)S(1)} %bitcast.451, pred[8192]{0:T(1024)(128)(4,1)S(1)} %get-tuple-element.339, pred[8192]{0:T(1024)(128)(4,1)S(1)} %get-tuple-element.338, ...), kind=kLoop, calls=%fused_computation.59 | loop fusion | flops 83886080 | bytes 16871424 | tf_op jit(solution)/shard_map/and | solution.py:34
  116.7 50.0 %fusion.20 = (f32[4,1024]{1,0:T(4,128)S(1)}, f32[4,1024,8192]{2,1,0:T(8,128)}) fusion(pred[1024,8192]{1,0:T(8,128)(4,1)} %get-tuple-element.451, bf16[1024,4,64]{0,2,1:T(8,128)(2,1)S(1)} %get-tuple-element.729, bf16[8192,4,64]{0,2,1:T(8,128)(2,1)} %bitcast.448), kind=kOutput, calls=%fused_computation.42 | convolution fusion | flops 4395626496 | bytes 147341312 | tf_op jit(solution)/shard_map/qhd,khd->hqk/dot_general | solution.py:106
  166.8 50.2 %fusion.21 = (f32[4,1024]{1,0:T(4,128)S(1)}, f32[4,1024,8192]{2,1,0:T(8,128)}) fusion(pred[1024,8192]{1,0:T(8,128)(4,1)} %get-tuple-element.450, bf16[1024,4,64]{0,2,1:T(8,128)(2,1)S(1)} %get-tuple-element.672, bf16[8192,4,64]{0,2,1:T(8,128)(2,1)} %bitcast.445), kind=kOutput, calls=%fused_computation.43 | convolution fusion | flops 4395626496 | bytes 147341312 | tf_op jit(solution)/shard_map/qhd,khd->hqk/dot_general | solution.py:106
  217.6 44.0 %fusion.22 = f32[4,1024]{1,0:T(4,128)S(1)} fusion(f32[4,1024,8192]{2,1,0:T(8,128)} %get-tuple-element.459, f32[4,1024]{1,0:T(4,128)S(1)} %broadcast_maximum_fusion.1, pred[1024,8192]{1,0:T(8,128)(4,1)} %get-tuple-element.451), kind=kLoop, calls=%fused_computation.44 | loop fusion | flops 167768064 | bytes 142639104 | tf_op jit(solution)/shard_map/reduce_sum | solution.py:117
  261.7 51.2 %divide_convert_fusion.1 = bf16[1024,4,64]{0,2,1:T(8,128)(2,1)S(1)} fusion(bf16[8192,4,64]{0,2,1:T(8,128)(2,1)} %bitcast.450, f32[4,1024,8192]{2,1,0:T(8,128)} %get-tuple-element.459, f32[4,1024]{1,0:T(4,128)S(1)} %broadcast_maximum_fusion.1, pred[1024,8192]{1,0:T(8,128)(4,1)} %get-tuple-element.451, f32[1024,4]{0,1:T(4,128)S(1)} %bitcast.460), kind=kOutput, calls=%fused_computation.207 | convolution fusion | flops 4463263744 | bytes 147357696 | tf_op jit(solution)/shard_map/hqk,khd->hqd/dot_general | solution.py:118
  314.3 43.9 %fusion.24 = f32[4,1024]{1,0:T(4,128)S(1)} fusion(f32[4,1024,8192]{2,1,0:T(8,128)} %get-tuple-element.461, f32[4,1024]{1,0:T(4,128)S(1)} %broadcast_maximum_fusion, pred[1024,8192]{1,0:T(8,128)(4,1)} %get-tuple-element.450), kind=kLoop, calls=%fused_computation.46 | loop fusion | flops 167768064 | bytes 142639104 | tf_op jit(solution)/shard_map/reduce_sum | solution.py:117
  358.2 51.0 %divide_convert_fusion = bf16[1024,4,64]{0,2,1:T(8,128)(2,1)} fusion(bf16[8192,4,64]{0,2,1:T(8,128)(2,1)} %bitcast.447, f32[4,1024,8192]{2,1,0:T(8,128)} %get-tuple-element.461, f32[4,1024]{1,0:T(4,128)S(1)} %broadcast_maximum_fusion, pred[1024,8192]{1,0:T(8,128)(4,1)} %get-tuple-element.450, f32[1024,4]{0,1:T(4,128)S(1)} %bitcast.459), kind=kOutput, calls=%fused_computation.205 | convolution fusion | flops 4463263744 | bytes 147357696 | tf_op jit(solution)/shard_map/hqk,khd->hqd/dot_general | solution.py:118
  412.2 21.7 %all-reduce.16.cloned.1.call-done = (bf16[1024,512]{1,0:T(8,128)(2,1)}, bf16[1024,512]{1,0:T(8,128)(2,1)}) async-done(((bf16[1024,512]{1,0:T(8,128)(2,1)}, bf16[1024,512]{1,0:T(8,128)(2,1)}), (bf16[1024,512]{1,0:T(8,128)(2,1)}, bf16[1024,512]{1,0:T(8,128)(2,1)})) %all-reduce.16.cloned.1.call-update) | async-done | bytes 2097168 | tf_op jit(solution)/shard_map/psum | solution.py:134
  439.4 5.0 multiply_convert_fusion.5
  462.7 15.1 all-reduce.14.cloned.1.call-done
  477.8 5.1 fusion.86
  493.0 300.7 %while.30 = (s32[]{:T(128)}, f32[1024,4,64]{0,2,1:T(8,128)S(1)}, f32[16,512,256]{1,2,0:T(8,128)}, bf16[16,512,256]{1,2,0:T(8,128)(2,1)}, s32[16]{0:T(128)S(1)}, ...) while((s32[]{:T(128)}, f32[1024,4,64]{0,2,1:T(8,128)S(1)}, ...), condition=%wide.region_21.22_spmd.clone, body=%wide.region_20.21_spmd.clone.sunk | while | flops 1366820864 | bytes 135865776 | solution.py:234
  793.7 6.9 copy.56
  801.3 6.6 multiply_convert_fusion.1
  808.0 6.3 copy.55
  821.6 302.6 %while.31 = (s32[]{:T(128)}, f32[1024,4,64]{0,2,1:T(8,128)S(1)}, f32[16,512,256]{1,2,0:T(8,128)}, bf16[16,512,256]{1,2,0:T(8,128)(2,1)}, s32[16]{0:T(128)S(1)}, ...) while((s32[]{:T(128)}, f32[1024,4,64]{0,2,1:T(8,128)S(1)}, ...), condition=%wide.region_32.33_spmd.clone, body=%wide.region_31.32_spmd.clone.sunk | while | flops 1366820864 | bytes 135865776 | solution.py:234
  826.9 4.7 fusion.263
  865.0 4.7 fusion.263
  940.8 4.7 fusion.263
  978.7 4.7 fusion.263
  1073.0 4.7 fusion.263
  1124.2 6.8 copy.59
  1131.1 6.6 multiply_convert_fusion
  1137.7 6.4 copy.58
  1170.8 49.7 %reduce-scatter.11.cloned.1.call-done = bf16[1024,256]{1,0:T(8,128)(2,1)} async-done(((bf16[8192,256]{1,0:T(8,128)(2,1)}), bf16[1024,256]{1,0:T(8,128)(2,1)}) %reduce-scatter.11.cloned.1.call-update) | async-done | bytes 524304 | tf_op jit(solution)/shard_map/reduce_scatter | solution.py:243
  1220.4 91.7 %reduce-scatter.9.cloned.1.call-done = bf16[1024,256]{1,0:T(8,128)(2,1)} async-done(((bf16[8192,256]{1,0:T(8,128)(2,1)}), bf16[1024,256]{1,0:T(8,128)(2,1)}) %reduce-scatter.9.cloned.1.call-update) | async-done | bytes 524304 | tf_op jit(solution)/shard_map/reduce_scatter | solution.py:240
  1331.9 134.7 %all-reduce.10.cloned.1.call-done = (bf16[3,512,256]{1,2,0:T(8,128)(2,1)}, bf16[256,512]{1,0:T(8,128)(2,1)}, bf16[512,1024]{1,0:T(8,128)(2,1)}, bf16[1024,512]{1,0:T(8,128)(2,1)}) async-done(((bf16[3,512,256]{1,2,0:T(8,128)(2,1)}, bf16[256,512]{1,0:T(8,128)(2,1)}, bf16[512,1024]{1,0:T(8,128)(2,1)}, bf16[1024,512]{1,0:T(8,128)(2,1)}), (bf16[3,512,256]{1,2,0:T(8,128)(2,1)}, bf16[256,512]{1,0:T(8,128)(2,1)}, ...) | async-done | bytes 3145744 | tf_op jit(solution)/shard_map/psum | solution.py:274
  1474.4 23.3 %all-reduce.12.cloned.1.call-done = (bf16[1024,512]{1,0:T(8,128)(2,1)}, bf16[1024,512]{1,0:T(8,128)(2,1)}, bf16[1024,512]{1,0:T(8,128)(2,1)}, bf16[1024,512]{1,0:T(8,128)(2,1)}) async-done(((bf16[1024,512]{1,0:T(8,128)(2,1)}, bf16[1024,512]{1,0:T(8,128)(2,1)}, bf16[1024,512]{1,0:T(8,128)(2,1)}, bf16[1024,512]{1,0:T(8,128)(2,1)}), (bf16[1024,512]{1,0:T(8,128)(2,1)}, bf16[1024,512]{1,0:T(8,128)(2,1)}, ...) | async-done | bytes 4194320 | tf_op jit(solution)/shard_map/psum | solution.py:142
  1497.7 6.0 fusion.87
  1503.8 42.9 %all-reduce = (bf16[512]{0:T(512)(128)(2,1)S(1)}, bf16[512]{0:T(512)(128)(2,1)S(1)}, bf16[2,256]{1,0:T(2,128)(2,1)S(1)}, bf16[512]{0:T(512)(128)(2,1)S(1)}, bf16...) all-reduce(bf16[512]{0:T(512)(128)(2,1)S(1)} %add_convert_fusion.15, ...), channel_id=1, replica_groups=mesh['dp'=2,'seq'=8,'tensor'=2] {'dp','seq'}, use_global_device_ids=true, to_apply=%region_40.41 | all-reduce | flops 4608 | bytes 18432 | tf_op jit(solution)/shard_map/psum | solution.py:272
  (1108 shorter events, 690.9 us)
Async XLA Ops:
  7.2 430.6 %copy-start = (bf16[512,1024]{1,0:T(8,128)(2,1)S(1)}, bf16[512,1024]{1,0:T(8,128)(2,1)}, u32[]{:S(2)}) copy-start(bf16[512,1024]{1,0:T(8,128)(2,1)} %param.32) | copy-start | bytes 3145732
  7.2 109.5 %all-gather.11.cloned.1.call-start = ((), (), s32[]{:S(2)}) async-start(), calls=%async_computation.10 | async-start | bytes 4718592 | tf_op jit(solution)/shard_map/all_gather | solution.py:98
  14.5 152.3 %all-gather.13.cloned.1.call-start = ((), (), s32[]{:S(2)}) async-start(), calls=%async_computation.11 | async-start | bytes 4718592 | tf_op jit(solution)/shard_map/all_gather | solution.py:98
  19.6 242.0 %all-gather.7.cloned.1.call-start = ((), (), s32[]{:S(2)}) async-start(), calls=%async_computation.4 | async-start | bytes 4718592 | tf_op jit(solution)/shard_map/all_gather | solution.py:99
  22.4 335.8 %all-gather.9.cloned.1.call-start = ((), (), s32[]{:S(2)}) async-start(), calls=%async_computation.5 | async-start | bytes 4718592 | tf_op jit(solution)/shard_map/all_gather | solution.py:99
  23.0 410.8 %all-reduce.16.cloned.1.call-start = ((), (), s32[]{:S(2)}) async-start(), calls=%async_computation.15 | async-start | bytes 4194304 | tf_op jit(solution)/shard_map/psum | solution.py:134
  55.8 36.3 %copy-start.54 = (s32[1,1024]{1,0:T(1,128)}, s32[1,1024]{1,0:T(1,128)S(1)}, u32[]{:S(2)}) copy-start(s32[1,1024]{1,0:T(1,128)S(1)} %get-tuple-element.669) | copy-start | bytes 12292
  55.8 36.3 %copy-start.56 = (s32[1,1024]{1,0:T(1,128)}, s32[1,1024]{1,0:T(1,128)S(1)}, u32[]{:S(2)}) copy-start(s32[1,1024]{1,0:T(1,128)S(1)} %get-tuple-element.726) | copy-start | bytes 12292
  55.8 34.9 %slice-start = ((f32[3,1024,256]{1,2,0:T(8,128)}), f32[1,1024,256]{1,2,0:T(8,128)S(1)}, s32[]{:S(2)}) async-start(f32[3,1024,256]{1,2,0:T(8,128)} %copy-done.36), calls=%async_computation.16 | async-start | bytes 2097152 | tf_op jit(solution)/shard_map/slice | solution.py:93
  58.3 58.4 %copy-start.58 = (s32[1,8192]{1,0:T(1,128)}, s32[1,8192]{1,0:T(1,128)S(1)}, u32[]{:S(2)}) copy-start(s32[1,8192]{1,0:T(1,128)S(1)} %get-tuple-element.444) | copy-start | bytes 98308
  58.3 58.4 %copy-start.59 = (s32[1,8192]{1,0:T(1,128)}, s32[1,8192]{1,0:T(1,128)S(1)}, u32[]{:S(2)}) copy-start(s32[1,8192]{1,0:T(1,128)S(1)} %get-tuple-element.445) | copy-start | bytes 98308
  92.1 24.6 %copy-start.16 = (bf16[1024,4,64]{0,2,1:T(8,128)(2,1)}, bf16[1024,4,64]{0,2,1:T(8,128)(2,1)S(1)}, u32[]{:S(2)}) copy-start(bf16[1024,4,64]{0,2,1:T(8,128)(2,1)S(1)} %get-tuple-element.729) | copy-start | bytes 1572868
  92.1 74.7 %copy-start.14 = (bf16[1024,4,64]{0,2,1:T(8,128)(2,1)}, bf16[1024,4,64]{0,2,1:T(8,128)(2,1)S(1)}, u32[]{:S(2)}) copy-start(bf16[1024,4,64]{0,2,1:T(8,128)(2,1)S(1)} %get-tuple-element.672) | copy-start | bytes 1572868
  166.7 50.3 %copy-start.68 = (f32[4,1024]{1,0:T(4,128)}, f32[4,1024]{1,0:T(4,128)S(1)}, u32[]{:S(2)}) copy-start(f32[4,1024]{1,0:T(4,128)S(1)} %get-tuple-element.458) | copy-start | bytes 49156
  261.6 51.2 %copy-start.64 = (f32[4,1024]{1,0:T(4,128)}, f32[4,1024]{1,0:T(4,128)S(1)}, u32[]{:S(2)}) copy-start(f32[4,1024]{1,0:T(4,128)S(1)} %fusion.22) | copy-start | bytes 49156
  261.7 51.2 %copy-start.37 = (bf16[256,512]{1,0:T(8,128)(2,1)S(1)}, bf16[256,512]{1,0:T(8,128)(2,1)}, u32[]{:S(2)}) copy-start(bf16[256,512]{1,0:T(8,128)(2,1)} %param.28) | copy-start | bytes 786436
  312.8 45.4 %copy-start.32 = (bf16[1024,4,64]{0,2,1:T(8,128)(2,1)}, bf16[1024,4,64]{0,2,1:T(8,128)(2,1)S(1)}, u32[]{:S(2)}) copy-start(bf16[1024,4,64]{0,2,1:T(8,128)(2,1)S(1)} %divide_convert_fusion.1) | copy-start | bytes 1572868
  409.2 24.6 %copy-start.74 = (f32[512]{0:T(512)S(1)}, f32[512]{0:T(512)}, u32[]{:S(2)}) copy-start(f32[512]{0:T(512)} %param.29) | copy-start | bytes 6148
  411.9 65.9 %all-reduce.14.cloned.1.call-start = ((), (), s32[]{:S(2)}) async-start(), calls=%async_computation.14 | async-start | bytes 4194304 | tf_op jit(solution)/shard_map/psum | solution.py:156
  436.3 46.7 %copy-start.72 = (f32[1024]{0:T(1024)}, f32[1024]{0:T(1024)S(1)}, u32[]{:S(2)}) copy-start(f32[1024]{0:T(1024)S(1)} %broadcast_multiply_fusion.10) | copy-start | bytes 12292
  436.3 46.6 %copy-start.70 = (f32[1024]{0:T(1024)}, f32[1024]{0:T(1024)S(1)}, u32[]{:S(2)}) copy-start(f32[1024]{0:T(1024)S(1)} %broadcast_multiply_fusion.8) | copy-start | bytes 12292
  437.8 45.2 %copy-start.80 = (f32[1024]{0:T(1024)}, f32[1024]{0:T(1024)S(1)}, u32[]{:S(2)}) copy-start(f32[1024]{0:T(1024)S(1)} %add_rsqrt_fusion) | copy-start | bytes 12292
  437.8 45.1 %copy-start.82 = (f32[1024]{0:T(1024)}, f32[1024]{0:T(1024)S(1)}, u32[]{:S(2)}) copy-start(f32[1024]{0:T(1024)S(1)} %add_rsqrt_fusion.2) | copy-start | bytes 12292
  455.1 711.9 %reduce-scatter.7.cloned.1.call-start = ((), (), s32[]{:S(2)}) async-start(), calls=%async_computation.7 | async-start | bytes 4718592 | tf_op jit(solution)/shard_map/reduce_scatter | solution.py:243
  800.6 366.4 %reduce-scatter.5.cloned.1.call-start = ((), (), s32[]{:S(2)}) async-start(), calls=%async_computation.6 | async-start | bytes 4718592 | tf_op jit(solution)/shard_map/reduce_scatter | solution.py:240
  817.2 403.2 %reduce-scatter.11.cloned.1.call-start = ((), (), s32[]{:S(2)}) async-start(), calls=%async_computation.9 | async-start | bytes 4718592 | tf_op jit(solution)/shard_map/reduce_scatter | solution.py:243
  1131.1 181.1 %reduce-scatter.9.cloned.1.call-start = ((), (), s32[]{:S(2)}) async-start(), calls=%async_computation.8 | async-start | bytes 4718592 | tf_op jit(solution)/shard_map/reduce_scatter | solution.py:240
  1144.1 322.5 %all-reduce.10.cloned.1.call-start = ((), (), s32[]{:S(2)}) async-start(), calls=%async_computation.12 | async-start | bytes 6291456 | tf_op jit(solution)/shard_map/psum | solution.py:274
  1167.0 145.2 %copy-start.61 = (f32[1024]{0:T(1024)S(1)}, f32[1024]{0:T(1024)}, u32[]{:S(2)}) copy-start(f32[1024]{0:T(1024)} %copy-done.60) | copy-start | bytes 12292
  1167.0 145.1 %copy-start.79 = (f32[1024]{0:T(1024)S(1)}, f32[1024]{0:T(1024)}, u32[]{:S(2)}) copy-start(f32[1024]{0:T(1024)} %copy-done.78) | copy-start | bytes 12292
  1316.2 181.5 %all-reduce.12.cloned.1.call-start = ((), (), s32[]{:S(2)}) async-start(), calls=%async_computation.13 | async-start | bytes 8388608 | tf_op jit(solution)/shard_map/psum | solution.py:142
  1472.8 24.9 %copy-start.98 = (f32[512]{0:T(512)S(1)}, f32[512]{0:T(512)}, u32[]{:S(2)}) copy-start(f32[512]{0:T(512)} %param.35) | copy-start | bytes 6148
  (248 other events, 976.0 us)
Sparse Core Ops, SparseCore 0:
  14.6 77.6 all-gather.10
  95.1 71.6 all-gather.12
  169.6 71.6 all-gather.6
  243.8 71.6 all-gather.8
  412.0 21.7 all-reduce.15
  455.3 22.4 all-reduce.13
  800.7 89.2 reduce-scatter.6
  894.1 87.8 reduce-scatter.4
  1131.2 89.2 reduce-scatter.10
  1224.3 87.7 reduce-scatter.8
  1318.7 147.7 all-reduce.9
  1470.0 27.6 all-reduce.11
where the time goes:
time: 1570 us
  matrix products  660 us (42%)
  waiting for transfers between devices  337 us (21%)
  local copies, waits for them, and re-layouts  215 us (14%)
  other arithmetic  207 us (13%)
  blocking collectives  107 us (7%)
  loops' own time  23.1 us (1%)
  between operations  15.8 us (1%)
    dot_general x32, matrix products, key_step(): jnp.einsum('qhd,khd->hqk', grad_heads, value_part, preferred_element_type...  148 us
    psum x1, waiting for transfers between devices, on_device(): lax.psum(sums[2].astype(jnp.bfloat16), ('dp', 'seq')).astype(jnp.float32)  135 us
    dot_general x32, matrix products, key_step(): jnp.einsum('hqk,khd->qhd', grad_scores, key_part, preferred_element_type=...  105 us
    dot_general x2, matrix products, on_device(): jnp.einsum('hqk,khd->hqd', weights.astype(jnp.bfloat16), value_part.resha...  102 us
    dot_general x2, matrix products, on_device(): jnp.einsum('qhd,khd->hqk', query_heads, key_part.reshape(row_count, heads...  100 us
    reduce_scatter x2, waiting for transfers between devices, on_device(): lax.psum_scatter(key_terms.astype(jnp.bfloat16), 'seq', scatter_dimension...  91.7 us
    reduce_sum x2, other arithmetic, on_device(): weight_sum = jnp.sum(weights, -1)  87.9 us
    dot_general x32, matrix products, key_step(): jnp.einsum('hqk,qhd->khd', probs.astype(jnp.bfloat16), grad_heads, prefer...  58.4 us
  transfers between devices with their start and end apart: 12, of which 7 were waited for; matrix products, arithmetic and copies ran while one was open for 41% of the time, Pallas kernels for 0%

commit v1 on v0

--- a/solution.py
+++ b/solution.py
@@ -6,6 +6,35 @@
 HEAD_DIM = 64
 EPSILON = 1e-05
 MASKED = -1e30
+
+
+def resolve_the_samples(local_values, which_axis):
+    parts_out = lax.axis_index(which_axis)
+    r2 = lax.axis_size(which_axis)
+    carry_out, shaped, z2 = (r2, parts_out, local_values.shape[1])
+    buffer = [d * carry_out if nth == 1 else d for nth, d in enumerate(local_values.shape)]
+    mixed_arr = jnp.zeros(buffer, local_values.dtype)
+    extra = current_value = local_values
+    known = lax.dynamic_update_slice_in_dim(mixed_arr, local_values, shaped * z2, axis=1)
+    for ii in range(1, carry_out // 2 + 1):
+        extra = lax.ppermute(
+            extra,
+            axis_name=which_axis,
+            perm=[(nth, (nth + 1) % carry_out) for nth in range(carry_out)],
+        )
+        known = lax.dynamic_update_slice_in_dim(
+            known, extra, (shaped - ii) % carry_out * z2, axis=1
+        )
+        if 2 * ii < carry_out:
+            current_value = lax.ppermute(
+                current_value,
+                axis_name=which_axis,
+                perm=[(nth, (nth - 1) % carry_out) for nth in range(carry_out)],
+            )
+            known = lax.dynamic_update_slice_in_dim(
+                known, current_value, (shaped + ii) % carry_out * z2, axis=1
+            )
+    return known
 
 
 def layer_norm(rows, gain, offset):
@@ -57,7 +86,7 @@
     heads_here = local_width // HEAD_DIM
     score_scale = HEAD_DIM ** (-0.5)
     seg_all, keep_all = (
-        lax.all_gather(segments, "seq", axis=1, tiled=True),
+        resolve_the_samples(segments, which_axis="seq"),
         lax.all_gather(keep_mask, "seq", axis=1, tiled=True),
     )
     full_length = seg_all.shape[1]

time: 1570 us -> 1570 us (level)
  blocking collectives: 107 us -> 73.9 us
  starting transfers between devices: 1.75 us -> 17.8 us
    all_gather x1 -> x0, blocking collectives: 32.7 us -> none  [on_device(): lax.all_gather(segments, 'seq', axis=1, tiled=True)]
    ppermute x0 -> x7, starting transfers between devices: none -> 16.1 us  [the longest x3 12.5 us: resolve_the_samples(): lax.ppermute(current_value, axis_name=which_axis, perm=[(nth, (nth - 1) %...]
  transfers between devices with their start and end apart: 12 -> 19, of which waited for: 7 -> 10; matrix products, arithmetic and copies ran while one was open for 41% -> 41% of each run, Pallas kernels for 0% -> 0%
where the time goes in v1:
time: 1570 us
  matrix products  660 us (42%)
  waiting for transfers between devices  352 us (22%)
  local copies, waits for them, and re-layouts  215 us (14%)
  other arithmetic  207 us (13%)
  blocking collectives  73.9 us (5%)
  loops' own time  22.9 us (1%)
  starting transfers between devices  17.8 us (1%)
  between operations  16 us (1%)
    dot_general x32, matrix products, key_step(): jnp.einsum('qhd,khd->hqk', grad_heads, value_part, preferred_element_type...  148 us
    psum x1, waiting for transfers between devices, on_device(): lax.psum(sums[2].astype(jnp.bfloat16), ('dp', 'seq')).astype(jnp.float32)  135 us
    dot_general x32, matrix products, key_step(): jnp.einsum('hqk,khd->qhd', grad_scores, key_part, preferred_element_type=...  106 us
    dot_general x2, matrix products, on_device(): jnp.einsum('hqk,khd->hqd', weights.astype(jnp.bfloat16), value_part.resha...  102 us
    dot_general x2, matrix products, on_device(): jnp.einsum('qhd,khd->hqk', query_heads, key_part.reshape(row_count, heads...  100 us
    reduce_scatter x2, waiting for transfers between devices, on_device(): lax.psum_scatter(key_terms.astype(jnp.bfloat16), 'seq', scatter_dimension...  91.6 us
    reduce_sum x2, other arithmetic, on_device(): weight_sum = jnp.sum(weights, -1)  88 us
    dot_general x32, matrix products, key_step(): jnp.einsum('hqk,qhd->khd', probs.astype(jnp.bfloat16), grad_heads, prefer...  58.4 us
  transfers between devices with their start and end apart: 19, of which 10 were waited for; matrix products, arithmetic and copies ran while one was open for 41% of the time, Pallas kernels for 0%

profile of v1, /device:TPU:0, one launch (start us, length us, event | category | flops | bytes accessed | tf_op | source)
XLA Modules:
  0.0 1565.2 jit_solution(11156361678083689009)
XLA Ops:
  31.1 30.9 %all_gather.19 = s32[2,8192]{1,0:T(2,128)S(1)} all-gather(s32[2,1024]{1,0:T(2,128)S(1)} %copy-done.89), channel_id=1, replica_groups=mesh['dp'=2,'seq'=8,'tensor'=2] {'seq'}, dimensions={1}, use_global_device_ids=true | all-gather | bytes 73728 | tf_op jit(solution)/shard_map/all_gather | solution.py:90
  64.7 4.7 collective-permute-start.3
  71.2 4.7 collective-permute-start.5
  78.4 6.4 collective-permute-done.6
  84.9 24.5 %fusion.37 = (pred[1024,8192]{1,0:T(8,128)(4,1)}, pred[1024,8192]{1,0:T(8,128)(4,1)}) fusion(s32[8192]{0:T(1024)S(1)} %bitcast.455, s32[1024]{0:T(1024)S(1)} %iota_add_fusion.4, s32[1024]{0:T(1024)S(1)} %bitcast.451, pred[8192]{0:T(1024)(128)(4,1)S(1)} %get-tuple-element.339, pred[8192]{0:T(1024)(128)(4,1)S(1)} %get-tuple-element.338, ...), kind=kLoop, calls=%fused_computation.59 | loop fusion | flops 83886080 | bytes 16871424 | tf_op jit(solution)/shard_map/and | solution.py:63
  109.5 50.0 %fusion.20 = (f32[4,1024]{1,0:T(4,128)S(1)}, f32[4,1024,8192]{2,1,0:T(8,128)}) fusion(pred[1024,8192]{1,0:T(8,128)(4,1)} %get-tuple-element.451, bf16[1024,4,64]{0,2,1:T(8,128)(2,1)S(1)} %get-tuple-element.729, bf16[8192,4,64]{0,2,1:T(8,128)(2,1)} %bitcast.448), kind=kOutput, calls=%fused_computation.42 | convolution fusion | flops 4395626496 | bytes 147341312 | tf_op jit(solution)/shard_map/qhd,khd->hqk/dot_general | solution.py:135
  159.5 7.2 all-gather.13.cloned.1.call-done
  166.6 50.2 %fusion.21 = (f32[4,1024]{1,0:T(4,128)S(1)}, f32[4,1024,8192]{2,1,0:T(8,128)}) fusion(pred[1024,8192]{1,0:T(8,128)(4,1)} %get-tuple-element.450, bf16[1024,4,64]{0,2,1:T(8,128)(2,1)S(1)} %get-tuple-element.672, bf16[8192,4,64]{0,2,1:T(8,128)(2,1)} %bitcast.445), kind=kOutput, calls=%fused_computation.43 | convolution fusion | flops 4395626496 | bytes 147341312 | tf_op jit(solution)/shard_map/qhd,khd->hqk/dot_general | solution.py:135
  217.4 44.0 %fusion.22 = f32[4,1024]{1,0:T(4,128)S(1)} fusion(f32[4,1024,8192]{2,1,0:T(8,128)} %get-tuple-element.459, f32[4,1024]{1,0:T(4,128)S(1)} %broadcast_maximum_fusion.1, pred[1024,8192]{1,0:T(8,128)(4,1)} %get-tuple-element.451), kind=kLoop, calls=%fused_computation.44 | loop fusion | flops 167768064 | bytes 142639104 | tf_op jit(solution)/shard_map/reduce_sum | solution.py:146
  261.5 51.2 %divide_convert_fusion.1 = bf16[1024,4,64]{0,2,1:T(8,128)(2,1)S(1)} fusion(bf16[8192,4,64]{0,2,1:T(8,128)(2,1)} %bitcast.450, f32[4,1024,8192]{2,1,0:T(8,128)} %get-tuple-element.459, f32[4,1024]{1,0:T(4,128)S(1)} %broadcast_maximum_fusion.1, pred[1024,8192]{1,0:T(8,128)(4,1)} %get-tuple-element.451, f32[1024,4]{0,1:T(4,128)S(1)} %bitcast.460), kind=kOutput, calls=%fused_computation.207 | convolution fusion | flops 4463263744 | bytes 147357696 | tf_op jit(solution)/shard_map/hqk,khd->hqd/dot_general | solution.py:147
  314.2 43.9 %fusion.24 = f32[4,1024]{1,0:T(4,128)S(1)} fusion(f32[4,1024,8192]{2,1,0:T(8,128)} %get-tuple-element.461, f32[4,1024]{1,0:T(4,128)S(1)} %broadcast_maximum_fusion, pred[1024,8192]{1,0:T(8,128)(4,1)} %get-tuple-element.450), kind=kLoop, calls=%fused_computation.46 | loop fusion | flops 167768064 | bytes 142639104 | tf_op jit(solution)/shard_map/reduce_sum | solution.py:146
  358.2 51.0 %divide_convert_fusion = bf16[1024,4,64]{0,2,1:T(8,128)(2,1)} fusion(bf16[8192,4,64]{0,2,1:T(8,128)(2,1)} %bitcast.447, f32[4,1024,8192]{2,1,0:T(8,128)} %get-tuple-element.461, f32[4,1024]{1,0:T(4,128)S(1)} %broadcast_maximum_fusion, pred[1024,8192]{1,0:T(8,128)(4,1)} %get-tuple-element.450, f32[1024,4]{0,1:T(4,128)S(1)} %bitcast.459), kind=kOutput, calls=%fused_computation.205 | convolution fusion | flops 4463263744 | bytes 147357696 | tf_op jit(solution)/shard_map/hqk,khd->hqd/dot_general | solution.py:147
  412.1 20.3 %all-reduce.16.cloned.1.call-done = (bf16[1024,512]{1,0:T(8,128)(2,1)}, bf16[1024,512]{1,0:T(8,128)(2,1)}) async-done(((bf16[1024,512]{1,0:T(8,128)(2,1)}, bf16[1024,512]{1,0:T(8,128)(2,1)}), (bf16[1024,512]{1,0:T(8,128)(2,1)}, bf16[1024,512]{1,0:T(8,128)(2,1)})) %all-reduce.16.cloned.1.call-update) | async-done | bytes 2097168 | tf_op jit(solution)/shard_map/psum | solution.py:163
  438.0 5.0 multiply_convert_fusion.5
  461.3 15.1 all-reduce.14.cloned.1.call-done
  476.4 5.1 fusion.86
  491.6 300.5 %while.30 = (s32[]{:T(128)}, f32[1024,4,64]{0,2,1:T(8,128)S(1)}, f32[16,512,256]{1,2,0:T(8,128)}, bf16[16,512,256]{1,2,0:T(8,128)(2,1)}, s32[16]{0:T(128)S(1)}, ...) while((s32[]{:T(128)}, f32[1024,4,64]{0,2,1:T(8,128)S(1)}, ...), condition=%wide.region_21.22_spmd.clone, body=%wide.region_20.21_spmd.clone.sunk | while | flops 1366820864 | bytes 135865776 | solution.py:263
  792.1 6.8 copy.56
  799.6 6.7 multiply_convert_fusion.1
  806.3 6.4 copy.55
  820.0 302.8 %while.31 = (s32[]{:T(128)}, f32[1024,4,64]{0,2,1:T(8,128)S(1)}, f32[16,512,256]{1,2,0:T(8,128)}, bf16[16,512,256]{1,2,0:T(8,128)(2,1)}, s32[16]{0:T(128)S(1)}, ...) while((s32[]{:T(128)}, f32[1024,4,64]{0,2,1:T(8,128)S(1)}, ...), condition=%wide.region_32.33_spmd.clone, body=%wide.region_31.32_spmd.clone.sunk | while | flops 1366820864 | bytes 135865776 | solution.py:263
  1052.7 4.7 fusion.263
  1071.6 4.7 fusion.263
  1122.9 6.8 copy.59
  1129.7 6.6 multiply_convert_fusion
  1136.3 6.4 copy.58
  1169.5 49.4 %reduce-scatter.11.cloned.1.call-done = bf16[1024,256]{1,0:T(8,128)(2,1)} async-done(((bf16[8192,256]{1,0:T(8,128)(2,1)}), bf16[1024,256]{1,0:T(8,128)(2,1)}) %reduce-scatter.11.cloned.1.call-update) | async-done | bytes 524304 | tf_op jit(solution)/shard_map/reduce_scatter | solution.py:272
  1218.9 91.6 %reduce-scatter.9.cloned.1.call-done = bf16[1024,256]{1,0:T(8,128)(2,1)} async-done(((bf16[8192,256]{1,0:T(8,128)(2,1)}), bf16[1024,256]{1,0:T(8,128)(2,1)}) %reduce-scatter.9.cloned.1.call-update) | async-done | bytes 524304 | tf_op jit(solution)/shard_map/reduce_scatter | solution.py:269
  1330.1 134.9 %all-reduce.10.cloned.1.call-done = (bf16[3,512,256]{1,2,0:T(8,128)(2,1)}, bf16[256,512]{1,0:T(8,128)(2,1)}, bf16[512,1024]{1,0:T(8,128)(2,1)}, bf16[1024,512]{1,0:T(8,128)(2,1)}) async-done(((bf16[3,512,256]{1,2,0:T(8,128)(2,1)}, bf16[256,512]{1,0:T(8,128)(2,1)}, bf16[512,1024]{1,0:T(8,128)(2,1)}, bf16[1024,512]{1,0:T(8,128)(2,1)}), (bf16[3,512,256]{1,2,0:T(8,128)(2,1)}, bf16[256,512]{1,0:T(8,128)(2,1)}, ...) | async-done | bytes 3145744 | tf_op jit(solution)/shard_map/psum | solution.py:303
  1472.8 23.3 %all-reduce.12.cloned.1.call-done = (bf16[1024,512]{1,0:T(8,128)(2,1)}, bf16[1024,512]{1,0:T(8,128)(2,1)}, bf16[1024,512]{1,0:T(8,128)(2,1)}, bf16[1024,512]{1,0:T(8,128)(2,1)}) async-done(((bf16[1024,512]{1,0:T(8,128)(2,1)}, bf16[1024,512]{1,0:T(8,128)(2,1)}, bf16[1024,512]{1,0:T(8,128)(2,1)}, bf16[1024,512]{1,0:T(8,128)(2,1)}), (bf16[1024,512]{1,0:T(8,128)(2,1)}, bf16[1024,512]{1,0:T(8,128)(2,1)}, ...) | async-done | bytes 4194320 | tf_op jit(solution)/shard_map/psum | solution.py:171
  1496.1 6.0 fusion.87
  1502.2 42.9 %all-reduce = (bf16[512]{0:T(512)(128)(2,1)S(1)}, bf16[512]{0:T(512)(128)(2,1)S(1)}, bf16[2,256]{1,0:T(2,128)(2,1)S(1)}, bf16[512]{0:T(512)(128)(2,1)S(1)}, bf16...) all-reduce(bf16[512]{0:T(512)(128)(2,1)S(1)} %add_convert_fusion.15, ...), channel_id=1, replica_groups=mesh['dp'=2,'seq'=8,'tensor'=2] {'dp','seq'}, use_global_device_ids=true, to_apply=%region_40.41 | all-reduce | flops 4608 | bytes 18432 | tf_op jit(solution)/shard_map/psum | solution.py:301
  (1130 shorter events, 714.9 us)
Async XLA Ops:
  7.2 429.2 %copy-start = (bf16[512,1024]{1,0:T(8,128)(2,1)S(1)}, bf16[512,1024]{1,0:T(8,128)(2,1)}, u32[]{:S(2)}) copy-start(bf16[512,1024]{1,0:T(8,128)(2,1)} %param.32) | copy-start | bytes 3145732
  7.2 102.2 %all-gather.11.cloned.1.call-start = ((), (), s32[]{:S(2)}) async-start(), calls=%async_computation.10 | async-start | bytes 4718592 | tf_op jit(solution)/shard_map/all_gather | solution.py:127
  14.5 152.2 %all-gather.13.cloned.1.call-start = ((), (), s32[]{:S(2)}) async-start(), calls=%async_computation.11 | async-start | bytes 4718592 | tf_op jit(solution)/shard_map/all_gather | solution.py:127
  19.6 241.9 %all-gather.7.cloned.1.call-start = ((), (), s32[]{:S(2)}) async-start(), calls=%async_computation.4 | async-start | bytes 4718592 | tf_op jit(solution)/shard_map/all_gather | solution.py:128
  22.4 335.8 %all-gather.9.cloned.1.call-start = ((), (), s32[]{:S(2)}) async-start(), calls=%async_computation.5 | async-start | bytes 4718592 | tf_op jit(solution)/shard_map/all_gather | solution.py:128
  22.5 42.1 %collective-permute-start = (s32[2,1024]{1,0:T(2,128)S(1)}, s32[2,1024]{1,0:T(2,128)S(1)}, u32[]{:S(2)}, u32[]{:S(2)}) collective-permute-start(s32[2,1024]{1,0:T(2,128)S(1)} %copy-done.84), channel_id=1, source_target_pairs={{0,2},{2,4},{4,6},{6,8},{8,10},{10,12},{12,14},{14,0},{1,3},{3,5},... | collective-permute-start | bytes 24584 | tf_op jit(solution)/shard_map/ppermute | solution.py:20
  25.5 39.2 %collective-permute-start.1 = (s32[2,1024]{1,0:T(2,128)S(1)}, s32[2,1024]{1,0:T(2,128)S(1)}, u32[]{:S(2)}, u32[]{:S(2)}) collective-permute-start(s32[2,1024]{1,0:T(2,128)S(1)} %copy-done.84), channel_id=1, source_target_pairs={{0,14},{2,0},{4,2},{6,4},{8,6},{10,8},{12,10},{14,12},{1,15},{3,1}... | collective-permute-start | bytes 24584 | tf_op jit(solution)/shard_map/ppermute | solution.py:29
  28.6 403.8 %all-reduce.16.cloned.1.call-start = ((), (), s32[]{:S(2)}) async-start(), calls=%async_computation.15 | async-start | bytes 4194304 | tf_op jit(solution)/shard_map/psum | solution.py:163
  28.7 56.2 %copy-start.54 = (s32[1,1024]{1,0:T(1,128)}, s32[1,1024]{1,0:T(1,128)S(1)}, u32[]{:S(2)}) copy-start(s32[1,1024]{1,0:T(1,128)S(1)} %get-tuple-element.669) | copy-start | bytes 12292
  28.7 56.2 %copy-start.56 = (s32[1,1024]{1,0:T(1,128)}, s32[1,1024]{1,0:T(1,128)S(1)}, u32[]{:S(2)}) copy-start(s32[1,1024]{1,0:T(1,128)S(1)} %get-tuple-element.726) | copy-start | bytes 12292
  64.4 102.2 %copy-start.14 = (bf16[1024,4,64]{0,2,1:T(8,128)(2,1)}, bf16[1024,4,64]{0,2,1:T(8,128)(2,1)S(1)}, u32[]{:S(2)}) copy-start(bf16[1024,4,64]{0,2,1:T(8,128)(2,1)S(1)} %get-tuple-element.672) | copy-start | bytes 1572868
  64.6 6.6 collective-permute-start.2
  64.7 6.6 collective-permute-start.3
  71.2 6.6 collective-permute-start.4
  71.2 7.1 collective-permute-start.5
  77.8 7.0 collective-permute-start.6
  159.4 57.4 %copy-start.68 = (f32[4,1024]{1,0:T(4,128)}, f32[4,1024]{1,0:T(4,128)S(1)}, u32[]{:S(2)}) copy-start(f32[4,1024]{1,0:T(4,128)S(1)} %get-tuple-element.458) | copy-start | bytes 49156
  261.5 51.3 %copy-start.64 = (f32[4,1024]{1,0:T(4,128)}, f32[4,1024]{1,0:T(4,128)S(1)}, u32[]{:S(2)}) copy-start(f32[4,1024]{1,0:T(4,128)S(1)} %fusion.22) | copy-start | bytes 49156
  261.5 51.2 %copy-start.37 = (bf16[256,512]{1,0:T(8,128)(2,1)S(1)}, bf16[256,512]{1,0:T(8,128)(2,1)}, u32[]{:S(2)}) copy-start(bf16[256,512]{1,0:T(8,128)(2,1)} %param.28) | copy-start | bytes 786436
  312.7 45.4 %copy-start.32 = (bf16[1024,4,64]{0,2,1:T(8,128)(2,1)}, bf16[1024,4,64]{0,2,1:T(8,128)(2,1)S(1)}, u32[]{:S(2)}) copy-start(bf16[1024,4,64]{0,2,1:T(8,128)(2,1)S(1)} %divide_convert_fusion.1) | copy-start | bytes 1572868
  411.8 64.5 %all-reduce.14.cloned.1.call-start = ((), (), s32[]{:S(2)}) async-start(), calls=%async_computation.14 | async-start | bytes 4194304 | tf_op jit(solution)/shard_map/psum | solution.py:185
  434.9 46.6 %copy-start.72 = (f32[1024]{0:T(1024)}, f32[1024]{0:T(1024)S(1)}, u32[]{:S(2)}) copy-start(f32[1024]{0:T(1024)S(1)} %broadcast_multiply_fusion.10) | copy-start | bytes 12292
  434.9 46.6 %copy-start.70 = (f32[1024]{0:T(1024)}, f32[1024]{0:T(1024)S(1)}, u32[]{:S(2)}) copy-start(f32[1024]{0:T(1024)S(1)} %broadcast_multiply_fusion.8) | copy-start | bytes 12292
  436.4 45.2 %copy-start.80 = (f32[1024]{0:T(1024)}, f32[1024]{0:T(1024)S(1)}, u32[]{:S(2)}) copy-start(f32[1024]{0:T(1024)S(1)} %add_rsqrt_fusion) | copy-start | bytes 12292
  453.7 712.0 %reduce-scatter.7.cloned.1.call-start = ((), (), s32[]{:S(2)}) async-start(), calls=%async_computation.7 | async-start | bytes 4718592 | tf_op jit(solution)/shard_map/reduce_scatter | solution.py:272
  798.9 366.8 %reduce-scatter.5.cloned.1.call-start = ((), (), s32[]{:S(2)}) async-start(), calls=%async_computation.6 | async-start | bytes 4718592 | tf_op jit(solution)/shard_map/reduce_scatter | solution.py:269
  815.6 403.3 %reduce-scatter.11.cloned.1.call-start = ((), (), s32[]{:S(2)}) async-start(), calls=%async_computation.9 | async-start | bytes 4718592 | tf_op jit(solution)/shard_map/reduce_scatter | solution.py:272
  1129.7 180.8 %reduce-scatter.9.cloned.1.call-start = ((), (), s32[]{:S(2)}) async-start(), calls=%async_computation.8 | async-start | bytes 4718592 | tf_op jit(solution)/shard_map/reduce_scatter | solution.py:269
  1142.7 322.2 %all-reduce.10.cloned.1.call-start = ((), (), s32[]{:S(2)}) async-start(), calls=%async_computation.12 | async-start | bytes 6291456 | tf_op jit(solution)/shard_map/psum | solution.py:303
  1165.7 144.8 %copy-start.61 = (f32[1024]{0:T(1024)S(1)}, f32[1024]{0:T(1024)}, u32[]{:S(2)}) copy-start(f32[1024]{0:T(1024)} %copy-done.60) | copy-start | bytes 12292
  1165.7 144.8 %copy-start.79 = (f32[1024]{0:T(1024)S(1)}, f32[1024]{0:T(1024)}, u32[]{:S(2)}) copy-start(f32[1024]{0:T(1024)} %copy-done.78) | copy-start | bytes 12292
  1314.5 181.6 %all-reduce.12.cloned.1.call-start = ((), (), s32[]{:S(2)}) async-start(), calls=%async_computation.13 | async-start | bytes 8388608 | tf_op jit(solution)/shard_map/psum | solution.py:171
  (255 other events, 1196.0 us)
Sparse Core Ops, SparseCore 0:
  14.6 77.4 all-gather.10
  94.8 71.7 all-gather.12
  169.4 71.6 all-gather.6
  243.7 71.6 all-gather.8
  411.9 20.4 all-reduce.15
  453.8 22.4 all-reduce.13
  799.0 89.2 reduce-scatter.6
  892.4 87.8 reduce-scatter.4
  1129.8 89.0 reduce-scatter.10
  1222.8 87.6 reduce-scatter.8
  1317.0 147.8 all-reduce.9
  1468.4 27.6 all-reduce.11
